TPU v7x, 128 devices: a whole 4x4x4 slice. The times are simulated.
128 devices in a mesh: dp: 8 (over z, core), mp: 16 (over y, x).
Axes of the slice: x: 4, y: 4, z: 4, core: 2. Of those that a mesh axis runs over, the one named last changes fastest.
Arguments:
- stream: bfloat16 [65536, 2048], P(('dp', 'mp')), may hold values from -5.5 to 5.5
- norm_weight: float32 [2048], replicated, may hold values from 0.5 to 1.5
- query_key_weight: bfloat16 [2048, 512], P(('dp', 'mp')), may hold values from -0.25 to 0.25
- value_weight: bfloat16 [2048, 2048], P(('dp', 'mp')), may hold values from -0.125 to 0.125
- output_weight: bfloat16 [2048, 2048], P(('dp', 'mp')), may hold values from -0.5 to 0.5
- convolution_weights: float32 [3, 2048], replicated, may hold values from -2.5 to 2.5
- adapter_down_maps: bfloat16 [64, 16, 2048], P('mp'), may hold values from -0.125 to 0.125
- adapter_up_maps: bfloat16 [64, 16, 2048], P('mp'), may hold values from -1.5 to 1.5
- prompt_lengths: int32 [128, 8], P(('dp', 'mp')), may hold values from 1 to 256, 512 in all within a row
- block_adapter_index: int32 [2048], P(('dp', 'mp')), may hold values from 0 to 63, as said below
Outputs:
- hidden: bfloat16 [65536, 2048], P(('dp', 'mp'))
Inputs may be any that keep to these rules, and one draw needn't show every extreme that they name: `prompt_lengths`: each row holds the lengths of one device's 8 prompts; a row sums to 512 and its largest entry is exactly 256. `block_adapter_index`: adapters k * 4 to (k + 1) * 4 - 1 sit on index k of mp. The 16 blocks of one device name adapters of any one index of mp at most 2 times; in every draw, on each index of dp, one index of mp is named exactly 2 times by every device.
All inputs are finite; a program needn't handle non-finite values.
Results may differ from a plain program's by a relative error of at most 0.0088.
Values may be sent and summed in bfloat16 or wider, within the bound.
A program may use at most 128 MiB of HBM per device.

v0:
```python
import math
import jax
import jax.numpy as jnp
from jax import lax
from jax.sharding import PartitionSpec as P

HEADS = 16
QK = 16
adapter_scale = 2.0
norm_eps = 1e-05


def prompt_index(lengths, total_token_count):
    bounds = jnp.cumsum(lengths)
    position = jnp.arange(total_token_count, dtype=jnp.int32)
    return jnp.sum((position[:, None] >= bounds[None, :]).astype(jnp.int32), axis=1)


def short_conv(value_matrix, tap_table, segment):
    result = tap_table[0][None, :] * value_matrix
    for offset in range(1, tap_table.shape[0]):
        earlier = jnp.concatenate(
            [jnp.zeros((offset, value_matrix.shape[1]), jnp.float32), value_matrix[:-offset]],
            axis=0,
        )
        same_prompt = jnp.concatenate(
            [jnp.zeros((offset,), jnp.bool_), segment[offset:] == segment[:-offset]], axis=0
        )
        result = result + tap_table[offset][None, :] * jnp.where(same_prompt[:, None], earlier, 0.0)
    return result


def taylor_heads(query_key, mixed, segment, head_count, feature):
    total_token_count, hidden_width = mixed.shape
    head_width = hidden_width // head_count
    queries = (
        query_key[:, : head_count * feature]
        .reshape(total_token_count, head_count, feature)
        .transpose(1, 0, 2)
    )
    key_rows = (
        query_key[:, head_count * feature :]
        .reshape(total_token_count, head_count, feature)
        .transpose(1, 0, 2)
    )
    value_rows = mixed.reshape(total_token_count, head_count, head_width).transpose(1, 0, 2)
    position = jnp.arange(total_token_count, dtype=jnp.int32)
    allowed = (position[None, :] <= position[:, None]) & (segment[None, :] == segment[:, None])
    score_scale = 1.0 / math.sqrt(feature)

    def one_head(operands):
        query_one, key_one, value_one = operands
        scores = jnp.dot(query_one, key_one.T, preferred_element_type=jnp.float32) * score_scale
        weight = jnp.where(allowed, 1.0 + scores + 0.5 * scores * scores, 0.0)
        row_total = jnp.sum(weight, axis=1, keepdims=True)
        numerator = jnp.dot(
            weight.astype(jnp.bfloat16), value_one, preferred_element_type=jnp.float32
        )
        return numerator / row_total

    outputs = lax.map(one_head, (queries, key_rows, value_rows))
    return outputs.transpose(1, 0, 2).reshape(total_token_count, hidden_width).astype(jnp.bfloat16)


def local(
    stream,
    norm_weight,
    query_key_weight,
    value_weight,
    output_weight,
    convolution_weights,
    adapter_down_maps,
    adapter_up_maps,
    prompt_lengths,
    block_adapter_index,
):
    total_token_count, hidden_width = stream.shape
    stream_f = stream.astype(jnp.float32)
    mean_sq = jnp.mean(stream_f * stream_f, axis=1, keepdims=True)
    normed = (stream_f * lax.rsqrt(mean_sq + norm_eps) * norm_weight[None, :]).astype(jnp.bfloat16)
    inputs = normed
    qk_sum = jnp.dot(
        inputs,
        lax.all_gather(query_key_weight, ("dp", "mp"), axis=0, tiled=True),
        preferred_element_type=jnp.float32,
    )
    plain_value_rows = jnp.dot(
        inputs,
        lax.all_gather(value_weight, ("dp", "mp"), axis=0, tiled=True),
        preferred_element_type=jnp.float32,
    )
    query_key = qk_sum.astype(jnp.bfloat16)
    holders = lax.axis_size("mp")
    local_token_count = adapter_down_maps.shape[0]
    adapter_width = adapter_down_maps.shape[1]
    block_count = block_adapter_index.shape[0]
    block_rows = total_token_count // block_count
    capacity = 2 * block_count // holders
    holder_of = block_adapter_index // local_token_count
    within = (block_adapter_index % local_token_count).astype(jnp.float32)
    onehot = (holder_of[:, None] == jnp.arange(holders, dtype=jnp.int32)[None, :]).astype(jnp.int32)
    slot_index = jnp.sum((jnp.cumsum(onehot, axis=0) - 1) * onehot, axis=1)
    target = holder_of * capacity + slot_index
    select = (jnp.arange(holders * capacity, dtype=jnp.int32)[:, None] == target[None, :]).astype(
        jnp.bfloat16
    )
    outgoing = jnp.dot(
        select,
        normed.reshape(block_count, block_rows * hidden_width),
        preferred_element_type=jnp.float32,
    )
    outgoing = outgoing.astype(jnp.bfloat16).reshape(holders, capacity * block_rows, hidden_width)
    slot_local = jnp.dot(select.astype(jnp.float32), within, preferred_element_type=jnp.float32)
    slot_local = (
        jnp.repeat(slot_local, block_rows)
        .astype(jnp.bfloat16)
        .reshape(holders, capacity * block_rows)
    )
    flattened_down = adapter_down_maps.reshape(local_token_count * adapter_width, hidden_width)
    flattened_up = adapter_up_maps.reshape(local_token_count * adapter_width, hidden_width)
    column_owner = (
        jnp.arange(local_token_count * adapter_width, dtype=jnp.int32) // adapter_width
    ).astype(jnp.float32)
    rows_here = lax.all_to_all(outgoing, "mp", split_axis=0, concat_axis=0, tiled=True)
    local_ids = lax.all_to_all(slot_local, "mp", split_axis=0, concat_axis=0, tiled=True)
    low_all = jnp.einsum(
        "skd,cd->skc", rows_here, flattened_down, preferred_element_type=jnp.float32
    )
    keep = local_ids.astype(jnp.float32)[:, :, None] == column_owner[None, None, :]
    reduced_rows = jnp.where(keep, low_all, 0.0).astype(jnp.bfloat16)
    value_update = adapter_scale * jnp.einsum(
        "skc,cd->skd", reduced_rows, flattened_up, preferred_element_type=jnp.float32
    )
    returned = lax.all_to_all(
        value_update.astype(jnp.bfloat16), "mp", split_axis=0, concat_axis=0, tiled=True
    )
    adapter_delta = jnp.dot(
        select.T,
        returned.reshape(holders * capacity, block_rows * hidden_width),
        preferred_element_type=jnp.float32,
    )
    adapter_delta = adapter_delta.reshape(total_token_count, hidden_width)
    value_matrix = plain_value_rows + adapter_delta
    segment = prompt_index(prompt_lengths[0], total_token_count)
    conv = short_conv(value_matrix, convolution_weights, segment)
    mixed = (conv * jax.nn.silu(value_matrix)).astype(jnp.bfloat16)
    attended = taylor_heads(query_key, mixed, segment, HEADS, QK)
    inputs = attended
    projected = jnp.dot(
        inputs,
        lax.all_gather(output_weight, ("dp", "mp"), axis=0, tiled=True),
        preferred_element_type=jnp.float32,
    )
    return (stream_f + projected).astype(jnp.bfloat16)


def solution(mesh):
    return jax.shard_map(
        local,
        mesh=mesh,
        in_specs=(
            P(("dp", "mp"), None),
            P(),
            P(("dp", "mp"), None),
            P(("dp", "mp"), None),
            P(("dp", "mp"), None),
            P(),
            P("mp", None, None),
            P("mp", None, None),
            P(("dp", "mp"), None),
            P(("dp", "mp")),
        ),
        out_specs=P(("dp", "mp"), None),
        check_vma=False,
    )
```

profile of v0, /device:TPU:1, one launch (start us, length us, event | category | flops | bytes accessed | tf_op | source)
XLA Modules:
  0.0 303.8 jit_solution(3091795847900209915)
XLA Ops:
  11.3 7.6 %all-to-all-start = ((bf16[16,1,64]{2,1,0:T(2,128)(2,1)}), bf16[16,1,64]{2,1,0:T(2,128)(2,1)S(1)}, u32[]{:S(2)}, u32[]{:S(2)}) async-start(bf16[16,1,64]{2,1,0:T(2,128)(2,1)} %convert_element_type.107), calls=%async_computation | async-start | bytes 16384 | tf_op jit(solution)/shard_map/all_to_all | solution.py:125
  18.9 2.1 fusion.13
  21.0 3.5 %fusion.15 = bf16[512,2048]{1,0:T(8,128)(2,1)} fusion(bf16[512,2048]{1,0:T(8,128)(2,1)} %param.12, f32[2048]{0:T(1024)} %param.13, f32[512]{0:T(512)S(1)} %add_rsqrt_fusion), kind=kLoop, calls=%fused_computation.23 | loop fusion | flops 4194304 | bytes 4204544 | tf_op jit(solution)/shard_map/convert_element_type | solution.py:80
  24.4 2.2 reshape.118
  26.6 3.2 %convolution_convert_fusion = bf16[32,65536]{1,0:T(8,128)(2,1)} fusion(bf16[16,65536]{1,0:T(8,128)(2,1)S(1)} %reshape.118, s32[16]{0:T(128)S(1)} %multiply_add_fusion), kind=kOutput, calls=%fused_computation.16 | convolution fusion | flops 69206528 | bytes 6291520 | tf_op jit(solution)/shard_map/dot_general | solution.py:107
  29.8 5.6 %reshape.119 = bf16[16,64,2048]{2,1,0:T(8,128)(2,1)} reshape(bf16[32,65536]{1,0:T(8,128)(2,1)} %convolution_convert_fusion) | data formatting | bytes 8388608 | tf_op jit(solution)/shard_map/reshape | solution.py:112
  35.5 6.8 %all-to-all-start.1 = ((bf16[16,64,2048]{2,1,0:T(8,128)(2,1)}), bf16[16,64,2048]{2,1,0:T(8,128)(2,1)}, u32[]{:S(2)}, u32[]{:S(2)}) async-start(bf16[16,64,2048]{2,1,0:T(8,128)(2,1)} %reshape.119), calls=%async_computation.1 | async-start | bytes 8388608 | tf_op jit(solution)/shard_map/all_to_all | solution.py:124
  43.1 61.8 %all-to-all-done.1 = bf16[16,64,2048]{2,1,0:T(8,128)(2,1)} async-done(((bf16[16,64,2048]{2,1,0:T(8,128)(2,1)}), bf16[16,64,2048]{2,1,0:T(8,128)(2,1)}, u32[]{:S(2)}, u32[]{:S(2)}) %all-to-all-start.1) | async-done | bytes 4194336 | tf_op jit(solution)/shard_map/all_to_all | solution.py:124
  104.8 8.5 %multiply_convert_fusion = bf16[16,64,2048]{2,1,0:T(8,128)(2,1)} fusion(bf16[64,2048,1]{1,0,2:T(8,128)(2,1)S(1)} %bitcast.74, bf16[16,64,2048]{2,1,0:T(8,128)(2,1)} %all-to-all-done.1, bf16[64,2048,1]{1,0,2:T(8,128)(2,1)S(1)} %bitcast.79, f32[64]{0:T(128)S(1)} %fusion.29, f32[16,64]{1,0:T(8,128)S(1)} %bitcast.83), kind=kOutput, calls=%fused_computation.17 | convolution fusion | flops 541261824 | bytes 8917248 | tf_op jit(solution)/shard_map/skc,cd->skd/dot_general | solution.py:131
  113.4 4.9 %all-to-all-start.2 = ((bf16[16,64,2048]{2,1,0:T(8,128)(2,1)}), bf16[16,64,2048]{2,1,0:T(8,128)(2,1)}, u32[]{:S(2)}, u32[]{:S(2)}) async-start(bf16[16,64,2048]{2,1,0:T(8,128)(2,1)} %multiply_convert_fusion), calls=%async_computation.2 | async-start | bytes 8388608 | tf_op jit(solution)/shard_map/all_to_all | solution.py:134
  118.9 2.9 convolution_convert_fusion.1
  121.9 53.5 %all-to-all-done.2 = bf16[16,64,2048]{2,1,0:T(8,128)(2,1)} async-done(((bf16[16,64,2048]{2,1,0:T(8,128)(2,1)}), bf16[16,64,2048]{2,1,0:T(8,128)(2,1)}, u32[]{:S(2)}, u32[]{:S(2)}) %all-to-all-start.2) | async-done | bytes 4194336 | tf_op jit(solution)/shard_map/all_to_all | solution.py:134
  175.3 5.7 %reshape.122 = bf16[32,65536]{1,0:T(8,128)(2,1)} reshape(bf16[16,64,2048]{2,1,0:T(8,128)(2,1)} %all-to-all-done.2) | data formatting | bytes 8388608 | tf_op jit(solution)/shard_map/reshape | solution.py:139
  181.0 5.0 %fusion.24 = f32[16,65536]{1,0:T(8,128)} fusion(bf16[32,65536]{1,0:T(8,128)(2,1)} %reshape.122, s32[16]{0:T(128)S(1)} %multiply_add_fusion), kind=kOutput, calls=%fused_computation.39 | convolution fusion | flops 67109376 | bytes 8388672 | tf_op jit(solution)/shard_map/dot_general | solution.py:137
  186.0 4.0 %reshape.123 = f32[512,2048]{1,0:T(8,128)} reshape(f32[16,65536]{1,0:T(8,128)} %fusion.24) | data formatting | bytes 8388608 | tf_op jit(solution)/shard_map/reshape | solution.py:142
  189.9 27.0 %all-gather.6.cloned.1.call-done = bf16[2048,2048]{1,0:T(8,128)(2,1)} async-done(((bf16[16,2048]{1,0:T(8,128)(2,1)}), bf16[2048,2048]{1,0:T(8,128)(2,1)}) %all-gather.6.cloned.1.call-update) | async-done | bytes 8388624 | tf_op jit(solution)/shard_map/all_gather | solution.py:89
  216.9 8.7 %convolution_add_fusion = f32[512,2048]{1,0:T(8,128)S(1)} fusion(f32[512,2048]{1,0:T(8,128)} %reshape.123, bf16[512,2048]{1,0:T(8,128)(2,1)S(1)} %copy-done.3, bf16[2048,2048]{1,0:T(8,128)(2,1)} %all-gather.6.cloned.1.call-done), kind=kOutput, calls=%fused_computation.26 | convolution fusion | flops 4296015872 | bytes 18874368 | tf_op jit(solution)/shard_map/dot_general | solution.py:87
  225.6 4.3 %bitcast_bitcast_fusion = bf16[16,512,128]{2,1,0:T(8,128)(2,1)} fusion(f32[512,2048]{1,0:T(8,128)S(1)} %convolution_add_fusion, f32[510,2048]{1,0:T(8,128)S(1)} %bitcast.75, pred[512]{0:T(512)(128)(4,1)S(1)} %concatenate.14, f32[2048]{0:T(1024)S(1)} %bitcast.81, f32[511,2048]{1,0:T(8,128)S(1)} %bitcast.76, pred[512]{0:T(512)(128)(4,1)S(1)} %pad_add_fusion, ...), kind=kLoop, calls=%fused_computation.27 | loop fusion | flops 13631488 | bytes 14681088 | tf_op jit(solution)/shard_map/transpose | solution.py:46
  230.0 40.6 %while.13 = (s32[]{:T(128)}, bf16[16,512,128]{1,2,0:T(8,128)(2,1)}, bf16[16,512,16]{1,2,0:T(8,128)(2,1)S(1)}, bf16[16,512,16]{1,2,0:T(8,128)(2,1)S(1)}, bf16[16,...) while((s32[]{:T(128)}, bf16[16,512,128]{1,2,0:T(8,128)(2,1)}, ...), condition=%wide.region_7.8_spmd.clone, body=%wide.region_5.7_spmd.clone.sunk | while | flops 78511616 | bytes 1878093 | solution.py:61
  230.4 1.4 fusion.61
  250.8 1.3 fusion.61
  255.9 1.3 fusion.61
  270.6 16.7 %all-gather.8.cloned.1.call-done = bf16[2048,2048]{1,0:T(8,128)(2,1)} async-done(((bf16[16,2048]{1,0:T(8,128)(2,1)}), bf16[2048,2048]{1,0:T(8,128)(2,1)}) %all-gather.8.cloned.1.call-update) | async-done | bytes 8388624 | tf_op jit(solution)/shard_map/all_gather | solution.py:151
  287.3 9.9 %fusion.16 = bf16[512,2048]{1,0:T(8,128)(2,1)} fusion(bf16[512,2048]{1,0:T(8,128)(2,1)S(1)} %copy-done.2, bf16[512,2048]{0,1:T(8,128)(2,1)} %bitcast.85, bf16[2048,2048]{1,0:T(8,128)(2,1)} %all-gather.8.cloned.1.call-done), kind=kOutput, calls=%fused_computation.24 | convolution fusion | flops 4298113024 | bytes 14680064 | tf_op jit(solution)/shard_map/dot_general | solution.py:149
  (104 shorter events, 42.7 us)
Async XLA Ops:
  6.5 98.3 %copy-start = (bf16[4,16,2048]{2,1,0:T(8,128)(2,1)S(1)}, bf16[4,16,2048]{2,1,0:T(8,128)(2,1)}, u32[]{:S(2)}) copy-start(bf16[4,16,2048]{2,1,0:T(8,128)(2,1)} %param.19) | copy-start | bytes 786436
  6.5 112.4 %all-gather.4.cloned.1.call-start = ((), (), s32[]{:S(2)}) async-start(), calls=%async_computation.3 | async-start | bytes 2113536 | tf_op jit(solution)/shard_map/all_gather | solution.py:84
  7.3 209.6 %all-gather.6.cloned.1.call-start = ((), (), s32[]{:S(2)}) async-start(), calls=%async_computation.4 | async-start | bytes 8454144 | tf_op jit(solution)/shard_map/all_gather | solution.py:89
  11.3 24.2 %all-to-all-start = ((bf16[16,1,64]{2,1,0:T(2,128)(2,1)}), bf16[16,1,64]{2,1,0:T(2,128)(2,1)S(1)}, u32[]{:S(2)}, u32[]{:S(2)}) async-start(bf16[16,1,64]{2,1,0:T(2,128)(2,1)} %convert_element_type.107), calls=%async_computation | async-start | bytes 16384 | tf_op jit(solution)/shard_map/all_to_all | solution.py:125
  35.4 69.4 %copy-start.4 = (bf16[4,16,2048]{2,1,0:T(8,128)(2,1)S(1)}, bf16[4,16,2048]{2,1,0:T(8,128)(2,1)}, u32[]{:S(2)}) copy-start(bf16[4,16,2048]{2,1,0:T(8,128)(2,1)} %param.18) | copy-start | bytes 786436
  35.5 69.4 %all-to-all-start.1 = ((bf16[16,64,2048]{2,1,0:T(8,128)(2,1)}), bf16[16,64,2048]{2,1,0:T(8,128)(2,1)}, u32[]{:S(2)}, u32[]{:S(2)}) async-start(bf16[16,64,2048]{2,1,0:T(8,128)(2,1)} %reshape.119), calls=%async_computation.1 | async-start | bytes 8388608 | tf_op jit(solution)/shard_map/all_to_all | solution.py:124
  42.3 245.0 %all-gather.8.cloned.1.call-start = ((), (), s32[]{:S(2)}) async-start(), calls=%async_computation.5 | async-start | bytes 8454144 | tf_op jit(solution)/shard_map/all_gather | solution.py:151
  113.4 4.9 %copy-start.6 = (s32[1,8]{1,0:T(1,128)S(1)}, s32[1,8]{1,0:T(1,128)}, u32[]{:S(2)}) copy-start(s32[1,8]{1,0:T(1,128)} %param.20) | copy-start | bytes 100
  113.4 5.5 %copy-start.5 = (f32[3,2048]{1,0:T(4,128)S(1)}, f32[3,2048]{1,0:T(4,128)}, u32[]{:S(2)}) copy-start(f32[3,2048]{1,0:T(4,128)} %param.17) | copy-start | bytes 73732
  113.4 5.5 %copy-start.3 = (bf16[512,2048]{1,0:T(8,128)(2,1)S(1)}, bf16[512,2048]{1,0:T(8,128)(2,1)}, u32[]{:S(2)}) copy-start(bf16[512,2048]{1,0:T(8,128)(2,1)} %fusion.15) | copy-start | bytes 6291460
  113.4 62.0 %all-to-all-start.2 = ((bf16[16,64,2048]{2,1,0:T(8,128)(2,1)}), bf16[16,64,2048]{2,1,0:T(8,128)(2,1)}, u32[]{:S(2)}, u32[]{:S(2)}) async-start(bf16[16,64,2048]{2,1,0:T(8,128)(2,1)} %multiply_convert_fusion), calls=%async_computation.2 | async-start | bytes 8388608 | tf_op jit(solution)/shard_map/all_to_all | solution.py:134
  230.0 57.3 %copy-start.2 = (bf16[512,2048]{1,0:T(8,128)(2,1)S(1)}, bf16[512,2048]{1,0:T(8,128)(2,1)}, u32[]{:S(2)}) copy-start(bf16[512,2048]{1,0:T(8,128)(2,1)} %param.12) | copy-start | bytes 6291460
  287.3 9.9 %copy-start.1 = (bf16[4,16,2048]{2,1,0:T(8,128)(2,1)S(1)}, bf16[4,16,2048]{2,1,0:T(8,128)(2,1)}, u32[]{:S(2)}) copy-start(bf16[4,16,2048]{2,1,0:T(8,128)(2,1)} %param.19) | copy-start | bytes 786436
Sparse Core Ops, SparseCore 0:
  10.3 105.3 all-gather.3
  118.9 97.9 all-gather.5
  220.0 67.2 all-gather.7
where the time goes:
time: 305 us; the launch traced here: 304 us
  waiting for transfers between devices  161 us (53%)
  matrix products  66.9 us (22%)
  local copies, waits for them, and re-layouts  31 us (10%)
  starting transfers between devices  19.4 us (6%)
  between operations  13.2 us (4%)
  other arithmetic  12 us (4%)
    all_to_all x1, waiting for transfers between devices, local(): lax.all_to_all(outgoing, 'mp', split_axis=0, concat_axis=0, tiled=True)  61.8 us
    all_to_all x1, waiting for transfers between devices, local(): lax.all_to_all(value_update.astype(jnp.bfloat16), 'mp', split_axis=0, con...  53.5 us
    all_gather x1, waiting for transfers between devices, local(): lax.all_gather(value_weight, ('dp', 'mp'), axis=0, tiled=True)  27 us
    dot_general x16, matrix products, one_head(): jnp.dot(weight.astype(jnp.bfloat16), value_one, preferred_element_type=jn...  20.4 us
    all_gather x1, waiting for transfers between devices, local(): lax.all_gather(output_weight, ('dp', 'mp'), axis=0, tiled=True)  16.7 us
    dynamic_update_slice x32, local copies, waits for them, and re-layouts, taylor_heads(): outputs = lax.map(one_head, (queries, key_rows, value_rows))  12.5 us
    dot_general x1, matrix products, local(): jnp.dot(inputs, lax.all_gather(output_weight, ('dp', 'mp'), axis=0, tiled...  9.94 us
    dot_general x1, matrix products, local(): jnp.dot(inputs, lax.all_gather(value_weight, ('dp', 'mp'), axis=0, tiled=...  8.73 us
  transfers between devices with their start and end apart: 6, of which 4 were waited for; matrix products, arithmetic and copies ran while one was open for 33% of the time, Pallas kernels for 0%

commit v1 on v0

--- a/solution.py
+++ b/solution.py
@@ -3,6 +3,7 @@
 import jax.numpy as jnp
 from jax import lax
 from jax.sharding import PartitionSpec as P
+from jax.lax import all_to_all, axis_size
 
 HEADS = 16
 QK = 16
@@ -84,10 +85,17 @@
         lax.all_gather(query_key_weight, ("dp", "mp"), axis=0, tiled=True),
         preferred_element_type=jnp.float32,
     )
+    show_shapes_in = lambda values, along_axis: jnp.concatenate(
+        all_to_all(
+            jnp.stack(axis_size(along_axis) * [values], 0),
+            axis_name=along_axis,
+            split_axis=0,
+            concat_axis=0,
+        ),
+        axis=0,
+    )
     plain_value_rows = jnp.dot(
-        inputs,
-        lax.all_gather(value_weight, ("dp", "mp"), axis=0, tiled=True),
-        preferred_element_type=jnp.float32,
+        inputs, show_shapes_in(value_weight, ("dp", "mp")), preferred_element_type=jnp.float32
     )
     query_key = qk_sum.astype(jnp.bfloat16)
     holders = lax.axis_size("mp")

time: 305 us -> 365 us (1.20)
  waiting for transfers between devices: 161 us -> 203 us
  starting transfers between devices: 19.4 us -> 31 us
  local copies, waits for them, and re-layouts: 31 us -> 35.2 us
    all_gather x1, waiting for transfers between devices: 0.02 us -> 77 us  [local(): lax.all_gather(query_key_weight, ('dp', 'mp'), axis=0, tiled=True)]
    all_gather x1 -> x0, waiting for transfers between devices: 27 us -> none  [local(): lax.all_gather(value_weight, ('dp', 'mp'), axis=0, tiled=True)]
    all_gather x1, waiting for transfers between devices: 16.7 us -> 2.73 us  [local(): lax.all_gather(output_weight, ('dp', 'mp'), axis=0, tiled=True)]
    all_to_all x0 -> x1, starting transfers between devices: none -> 11.5 us  [local(): all_to_all(jnp.stack(axis_size(along_axis) * [values], 0), axis_name=alon...]
    another operation x0 -> x1, local copies, waits for them, and re-layouts: none -> 4.29 us  [local(): jnp.stack(axis_size(along_axis) * [values], 0)]
    all_to_all x0 -> x1, waiting for transfers between devices: none -> 4.04 us  [local(): all_to_all(jnp.stack(axis_size(along_axis) * [values], 0), axis_name=alon...]
  transfers between devices with their start and end apart: 6 -> 6, of which waited for: 4 -> 5; matrix products, arithmetic and copies ran while one was open for 33% -> 26% of each run, Pallas kernels for 0% -> 0%
where the time goes in v1:
time: 365 us; the launch traced here: 362 us
  waiting for transfers between devices  203 us (56%)
  matrix products  67.1 us (18%)
  local copies, waits for them, and re-layouts  35.2 us (10%)
  starting transfers between devices  31 us (8%)
  between operations  13.5 us (4%)
  other arithmetic  12.1 us (3%)
    all_gather x1, waiting for transfers between devices, local(): lax.all_gather(query_key_weight, ('dp', 'mp'), axis=0, tiled=True)  77 us
    all_to_all x1, waiting for transfers between devices, local(): lax.all_to_all(outgoing, 'mp', split_axis=0, concat_axis=0, tiled=True)  60.9 us
    all_to_all x1, waiting for transfers between devices, local(): lax.all_to_all(value_update.astype(jnp.bfloat16), 'mp', split_axis=0, con...  56.9 us
    dot_general x16, matrix products, one_head(): jnp.dot(weight.astype(jnp.bfloat16), value_one, preferred_element_type=jn...  20.6 us
    dynamic_update_slice x32, local copies, waits for them, and re-layouts, taylor_heads(): outputs = lax.map(one_head, (queries, key_rows, value_rows))  12.4 us
    all_to_all x1, starting transfers between devices, local(): all_to_all(jnp.stack(axis_size(along_axis) * [values], 0), axis_name=alon...  11.5 us
    dot_general x1, matrix products, local(): jnp.dot(inputs, lax.all_gather(output_weight, ('dp', 'mp'), axis=0, tiled...  9.94 us
    dot_general x1, matrix products, local(): jnp.dot(inputs, show_shapes_in(value_weight, ('dp', 'mp')), preferred_ele...  8.76 us
  transfers between devices with their start and end apart: 6, of which 5 were waited for; matrix products, arithmetic and copies ran while one was open for 26% of the time, Pallas kernels for 0%

profile of v1, /device:TPU:1, one launch (start us, length us, event | category | flops | bytes accessed | tf_op | source)
XLA Modules:
  0.0 361.8 jit_solution(9743019757618046526)
XLA Ops:
  9.9 7.6 %all-to-all-start.1 = ((bf16[16,1,64]{2,1,0:T(2,128)(2,1)}), bf16[16,1,64]{2,1,0:T(2,128)(2,1)S(1)}, u32[]{:S(2)}, u32[]{:S(2)}) async-start(bf16[16,1,64]{2,1,0:T(2,128)(2,1)} %convert_element_type.107), calls=%async_computation.1 | async-start | bytes 16384 | tf_op jit(solution)/shard_map/all_to_all | solution.py:133
  17.4 2.1 fusion.13
  19.5 3.5 fusion.15
  23.0 2.2 reshape.124
  25.2 3.2 convolution_convert_fusion
  28.4 5.6 %reshape.125 = bf16[16,64,2048]{2,1,0:T(8,128)(2,1)} reshape(bf16[32,65536]{1,0:T(8,128)(2,1)} %convolution_convert_fusion) | data formatting | bytes 8388608 | tf_op jit(solution)/shard_map/reshape | solution.py:120
  34.1 6.8 %all-to-all-start.2 = ((bf16[16,64,2048]{2,1,0:T(8,128)(2,1)}), bf16[16,64,2048]{2,1,0:T(8,128)(2,1)}, u32[]{:S(2)}, u32[]{:S(2)}) async-start(bf16[16,64,2048]{2,1,0:T(8,128)(2,1)} %reshape.125), calls=%async_computation.2 | async-start | bytes 8388608 | tf_op jit(solution)/shard_map/all_to_all | solution.py:132
  40.9 60.9 %all-to-all-done.2 = bf16[16,64,2048]{2,1,0:T(8,128)(2,1)} async-done(((bf16[16,64,2048]{2,1,0:T(8,128)(2,1)}), bf16[16,64,2048]{2,1,0:T(8,128)(2,1)}, u32[]{:S(2)}, u32[]{:S(2)}) %all-to-all-start.2) | async-done | bytes 4194336 | tf_op jit(solution)/shard_map/all_to_all | solution.py:132
  101.8 8.5 %multiply_convert_fusion = bf16[16,64,2048]{2,1,0:T(8,128)(2,1)} fusion(bf16[64,2048,1]{1,0,2:T(8,128)(2,1)S(1)} %bitcast.75, bf16[16,64,2048]{2,1,0:T(8,128)(2,1)} %all-to-all-done.2, bf16[64,2048,1]{1,0,2:T(8,128)(2,1)S(1)} %bitcast.80, f32[64]{0:T(128)S(1)} %fusion.29, f32[16,64]{1,0:T(8,128)S(1)} %bitcast.84), kind=kOutput, calls=%fused_computation.17 | convolution fusion | flops 541261824 | bytes 8917248 | tf_op jit(solution)/shard_map/skc,cd->skd/dot_general | solution.py:139
  110.3 4.9 %all-to-all-start.3 = ((bf16[16,64,2048]{2,1,0:T(8,128)(2,1)}), bf16[16,64,2048]{2,1,0:T(8,128)(2,1)}, u32[]{:S(2)}, u32[]{:S(2)}) async-start(bf16[16,64,2048]{2,1,0:T(8,128)(2,1)} %multiply_convert_fusion), calls=%async_computation.3 | async-start | bytes 8388608 | tf_op jit(solution)/shard_map/all_to_all | solution.py:142
  115.9 56.9 %all-to-all-done.3 = bf16[16,64,2048]{2,1,0:T(8,128)(2,1)} async-done(((bf16[16,64,2048]{2,1,0:T(8,128)(2,1)}), bf16[16,64,2048]{2,1,0:T(8,128)(2,1)}, u32[]{:S(2)}, u32[]{:S(2)}) %all-to-all-start.3) | async-done | bytes 4194336 | tf_op jit(solution)/shard_map/all_to_all | solution.py:142
  172.7 4.3 %stack.2 = bf16[128,16,2048]{2,1,0:T(8,128)(2,1)} broadcast(bf16[16,2048]{1,0:T(8,128)(2,1)S(1)} %copy-done.5), dimensions={1,2} | broadcast | bytes 8454144 | tf_op jit(solution)/shard_map/stack | solution.py:90
  177.0 11.5 %all-to-all-start = ((bf16[128,16,2048]{2,1,0:T(8,128)(2,1)}), bf16[128,16,2048]{2,1,0:T(8,128)(2,1)}, u32[]{:S(2)}, u32[]{:S(2)}) async-start(bf16[128,16,2048]{2,1,0:T(8,128)(2,1)} %stack.2), calls=%async_computation | async-start | bytes 16777216 | tf_op jit(solution)/shard_map/all_to_all | solution.py:89
  189.9 77.0 %all-gather.3.cloned.1.call-done = bf16[2048,512]{1,0:T(8,128)(2,1)} async-done(((bf16[16,512]{1,0:T(8,128)(2,1)}), bf16[2048,512]{1,0:T(8,128)(2,1)}) %all-gather.3.cloned.1.call-update) | async-done | bytes 2097168 | tf_op jit(solution)/shard_map/all_gather | solution.py:85
  266.9 2.9 convolution_convert_fusion.1
  269.8 5.6 %reshape.128 = bf16[32,65536]{1,0:T(8,128)(2,1)} reshape(bf16[16,64,2048]{2,1,0:T(8,128)(2,1)} %all-to-all-done.3) | data formatting | bytes 8388608 | tf_op jit(solution)/shard_map/reshape | solution.py:147
  275.4 5.0 %fusion.24 = f32[16,65536]{1,0:T(8,128)} fusion(bf16[32,65536]{1,0:T(8,128)(2,1)} %reshape.128, s32[16]{0:T(128)S(1)} %multiply_add_fusion), kind=kOutput, calls=%fused_computation.39 | convolution fusion | flops 67109376 | bytes 8388672 | tf_op jit(solution)/shard_map/dot_general | solution.py:145
  280.4 4.0 %reshape.129 = f32[512,2048]{1,0:T(8,128)} reshape(f32[16,65536]{1,0:T(8,128)} %fusion.24) | data formatting | bytes 8388608 | tf_op jit(solution)/shard_map/reshape | solution.py:150
  284.4 4.0 %all-to-all-done = bf16[128,16,2048]{2,1,0:T(8,128)(2,1)} async-done(((bf16[128,16,2048]{2,1,0:T(8,128)(2,1)}), bf16[128,16,2048]{2,1,0:T(8,128)(2,1)}, u32[]{:S(2)}, u32[]{:S(2)}) %all-to-all-start) | async-done | bytes 8388640 | tf_op jit(solution)/shard_map/all_to_all | solution.py:89
  288.5 8.8 %convolution_add_fusion = f32[512,2048]{1,0:T(8,128)S(1)} fusion(f32[512,2048]{1,0:T(8,128)} %reshape.129, bf16[512,2048]{1,0:T(8,128)(2,1)S(1)} %copy-done.3, bf16[2048,2048]{1,0:T(8,128)(2,1)} %bitcast.5), kind=kOutput, calls=%fused_computation.26 | convolution fusion | flops 4296015872 | bytes 18874368 | tf_op jit(solution)/shard_map/dot_general | solution.py:97
  297.2 4.3 %bitcast_bitcast_fusion = bf16[16,512,128]{2,1,0:T(8,128)(2,1)} fusion(f32[512,2048]{1,0:T(8,128)S(1)} %convolution_add_fusion, f32[510,2048]{1,0:T(8,128)S(1)} %bitcast.76, pred[512]{0:T(512)(128)(4,1)S(1)} %concatenate.14, f32[2048]{0:T(1024)S(1)} %bitcast.82, f32[511,2048]{1,0:T(8,128)S(1)} %bitcast.77, pred[512]{0:T(512)(128)(4,1)S(1)} %pad_add_fusion, ...), kind=kLoop, calls=%fused_computation.27 | loop fusion | flops 13631488 | bytes 14681088 | tf_op jit(solution)/shard_map/transpose | solution.py:47
  301.6 40.7 %while.13 = (s32[]{:T(128)}, bf16[16,512,128]{1,2,0:T(8,128)(2,1)}, bf16[16,512,16]{1,2,0:T(8,128)(2,1)S(1)}, bf16[16,512,16]{1,2,0:T(8,128)(2,1)S(1)}, bf16[16,...) while((s32[]{:T(128)}, bf16[16,512,128]{1,2,0:T(8,128)(2,1)}, ...), condition=%wide.region_7.8_spmd.clone, body=%wide.region_5.7_spmd.clone.sunk | while | flops 78511616 | bytes 1878093 | solution.py:62
  342.3 2.7 all-gather.5.cloned.1.call-done
  345.0 9.9 %fusion.16 = bf16[512,2048]{1,0:T(8,128)(2,1)} fusion(bf16[512,2048]{1,0:T(8,128)(2,1)S(1)} %copy-done.2, bf16[512,2048]{0,1:T(8,128)(2,1)} %bitcast.86, bf16[2048,2048]{1,0:T(8,128)(2,1)} %all-gather.5.cloned.1.call-done), kind=kOutput, calls=%fused_computation.24 | convolution fusion | flops 4298113024 | bytes 14680064 | tf_op jit(solution)/shard_map/dot_general | solution.py:157
  (106 shorter events, 46.0 us)
Async XLA Ops:
  6.5 95.3 %copy-start = (bf16[4,16,2048]{2,1,0:T(8,128)(2,1)S(1)}, bf16[4,16,2048]{2,1,0:T(8,128)(2,1)}, u32[]{:S(2)}) copy-start(bf16[4,16,2048]{2,1,0:T(8,128)(2,1)} %param.19) | copy-start | bytes 786436
  9.9 24.2 %all-to-all-start.1 = ((bf16[16,1,64]{2,1,0:T(2,128)(2,1)}), bf16[16,1,64]{2,1,0:T(2,128)(2,1)S(1)}, u32[]{:S(2)}, u32[]{:S(2)}) async-start(bf16[16,1,64]{2,1,0:T(2,128)(2,1)} %convert_element_type.107), calls=%async_computation.1 | async-start | bytes 16384 | tf_op jit(solution)/shard_map/all_to_all | solution.py:133
  34.0 67.8 %copy-start.4 = (bf16[4,16,2048]{2,1,0:T(8,128)(2,1)S(1)}, bf16[4,16,2048]{2,1,0:T(8,128)(2,1)}, u32[]{:S(2)}) copy-start(bf16[4,16,2048]{2,1,0:T(8,128)(2,1)} %param.18) | copy-start | bytes 786436
  34.1 67.7 %all-to-all-start.2 = ((bf16[16,64,2048]{2,1,0:T(8,128)(2,1)}), bf16[16,64,2048]{2,1,0:T(8,128)(2,1)}, u32[]{:S(2)}, u32[]{:S(2)}) async-start(bf16[16,64,2048]{2,1,0:T(8,128)(2,1)} %reshape.125), calls=%async_computation.2 | async-start | bytes 8388608 | tf_op jit(solution)/shard_map/all_to_all | solution.py:132
  110.3 62.5 %copy-start.5 = (bf16[16,2048]{1,0:T(8,128)(2,1)S(1)}, bf16[16,2048]{1,0:T(8,128)(2,1)}, u32[]{:S(2)}) copy-start(bf16[16,2048]{1,0:T(8,128)(2,1)} %param.15) | copy-start | bytes 196612
  110.3 62.5 %all-to-all-start.3 = ((bf16[16,64,2048]{2,1,0:T(8,128)(2,1)}), bf16[16,64,2048]{2,1,0:T(8,128)(2,1)}, u32[]{:S(2)}, u32[]{:S(2)}) async-start(bf16[16,64,2048]{2,1,0:T(8,128)(2,1)} %multiply_convert_fusion), calls=%async_computation.3 | async-start | bytes 8388608 | tf_op jit(solution)/shard_map/all_to_all | solution.py:142
  115.1 151.7 %all-gather.3.cloned.1.call-start = ((), (), s32[]{:S(2)}) async-start(), calls=%async_computation.4 | async-start | bytes 2113536 | tf_op jit(solution)/shard_map/all_gather | solution.py:85
  177.0 12.2 %copy-start.7 = (s32[1,8]{1,0:T(1,128)S(1)}, s32[1,8]{1,0:T(1,128)}, u32[]{:S(2)}) copy-start(s32[1,8]{1,0:T(1,128)} %param.20) | copy-start | bytes 100
  177.0 12.8 %copy-start.6 = (f32[3,2048]{1,0:T(4,128)S(1)}, f32[3,2048]{1,0:T(4,128)}, u32[]{:S(2)}) copy-start(f32[3,2048]{1,0:T(4,128)} %param.17) | copy-start | bytes 73732
  177.0 89.8 %copy-start.3 = (bf16[512,2048]{1,0:T(8,128)(2,1)S(1)}, bf16[512,2048]{1,0:T(8,128)(2,1)}, u32[]{:S(2)}) copy-start(bf16[512,2048]{1,0:T(8,128)(2,1)} %fusion.15) | copy-start | bytes 6291460
  177.0 111.4 %all-to-all-start = ((bf16[128,16,2048]{2,1,0:T(8,128)(2,1)}), bf16[128,16,2048]{2,1,0:T(8,128)(2,1)}, u32[]{:S(2)}, u32[]{:S(2)}) async-start(bf16[128,16,2048]{2,1,0:T(8,128)(2,1)} %stack.2), calls=%async_computation | async-start | bytes 16777216 | tf_op jit(solution)/shard_map/all_to_all | solution.py:89
  188.5 156.5 %all-gather.5.cloned.1.call-start = ((), (), s32[]{:S(2)}) async-start(), calls=%async_computation.5 | async-start | bytes 8454144 | tf_op jit(solution)/shard_map/all_gather | solution.py:159
  301.6 43.5 %copy-start.2 = (bf16[512,2048]{1,0:T(8,128)(2,1)S(1)}, bf16[512,2048]{1,0:T(8,128)(2,1)}, u32[]{:S(2)}) copy-start(bf16[512,2048]{1,0:T(8,128)(2,1)} %param.12) | copy-start | bytes 6291460
  345.0 9.9 %copy-start.1 = (bf16[4,16,2048]{2,1,0:T(8,128)(2,1)S(1)}, bf16[4,16,2048]{2,1,0:T(8,128)(2,1)}, u32[]{:S(2)}) copy-start(bf16[4,16,2048]{2,1,0:T(8,128)(2,1)} %param.19) | copy-start | bytes 786436
Sparse Core Ops, SparseCore 0:
  118.9 147.8 all-gather.2
  270.0 74.9 all-gather.4
